TPU v7x, 128 devices: a whole 4x4x4 slice. The times are simulated.
128 devices in a mesh: row: 64 (over z, y, x), pan: 2 (over core).
Axes of the slice: x: 4, y: 4, z: 4, core: 2. Of those that a mesh axis runs over, the one named last changes fastest.
Arguments:
- right_side: float32 [256, 65536], P(None, 'row'), may hold values from -6 to 6
- initial_guess: float32 [256, 65536], P(None, ('row', 'pan')), may hold values from -6 to 6
- v_factor: float32 [128, 128, 16, 512], P('row', None, 'pan'), may hold values from -0.25 to 0.25
- u_factor: float32 [128, 128, 16, 512], P('row', None, 'pan'), may hold values from -0.125 to 0.125
- tile_ranks: int32 [128, 128], P(None, 'row'), may hold values from 0 to 16
- diag_block: float32 [65536, 512], P(('row', 'pan'))
- diag_inverse: float32 [65536, 512], P(('row', 'pan'))
Outputs:
- solution: float32 [256, 65536], P(None, ('row', 'pan'))
- residual: float32 [256, 65536], P(None, ('row', 'pan'))
Inputs may be any that keep to these rules, and one draw needn't show every extreme that they name: `tile_ranks`: columns of a tile's factors from its rank on are ignored, as is the low-rank part of tile (i, i).
All inputs are finite; a program needn't handle non-finite values.
Results may differ from a plain program's by a relative error of at most 0.00017.
Values sent between devices are 32-bit elements; how exact they have to be, the bound alone decides.
A program may use at most 64 MiB of HBM per device.

v0:
```python
import jax
import jax.numpy as jnp
from jax import lax
from jax.sharding import PartitionSpec as P

ITERS = 2


def on_device(right_side, initial_guess, v_factor, u_factor, tile_ranks, diag_block, diag_inverse):
    highest = lax.Precision.HIGHEST
    pan_index = lax.axis_index("pan")
    row_index = lax.axis_index("row")
    tile_rows = v_factor.shape[0]
    tile_count = v_factor.shape[1]
    part_rank = v_factor.shape[2]
    tile_width = v_factor.shape[3]
    rhs_count = right_side.shape[0]
    own_rows = diag_block.shape[0]
    row_start = pan_index * own_rows
    tile_slot = row_start // tile_width
    components = pan_index * part_rank + jnp.arange(part_rank, dtype=jnp.int32)
    own_columns = row_index * tile_rows + jnp.arange(tile_rows, dtype=jnp.int32)
    tile_index = jnp.arange(tile_count, dtype=jnp.int32)
    off_diagonal = tile_index[:, None] != own_columns[None, :]
    rank_mask = (
        (components[None, None, :] < tile_ranks[:, :, None]) & off_diagonal[:, :, None]
    ).astype(jnp.float32)
    iterate_rows = initial_guess
    residual = initial_guess
    for iteration in range(ITERS):
        guess_full = lax.all_gather(iterate_rows, "pan", axis=1, tiled=True)
        guess_tiles = guess_full.reshape(rhs_count, tile_rows, tile_width)
        projected = jnp.einsum("cikb,rcb->ickr", v_factor, guess_tiles, precision=highest)
        projected = projected * rank_mask[:, :, :, None]
        received = lax.all_to_all(projected, "row", split_axis=0, concat_axis=1, tiled=True)
        low_rank = jnp.einsum("ickm,ickr->rim", u_factor, received, precision=highest)
        low_rank = low_rank.reshape(rhs_count, tile_rows * tile_width)
        guess_tile = lax.dynamic_slice_in_dim(guess_full, tile_slot * tile_width, tile_width, 1)
        dense_part = jnp.einsum("rb,mb->rm", guess_tile, diag_block, precision=highest)
        low_rows = lax.psum_scatter(low_rank, "pan", scatter_dimension=1, tiled=True)
        rhs_rows = lax.dynamic_slice_in_dim(right_side, row_start, own_rows, 1)
        residual = rhs_rows - (dense_part + low_rows)
        residual_full = lax.all_gather(residual, "pan", axis=1, tiled=True)
        residual_tile = lax.dynamic_slice_in_dim(
            residual_full, tile_slot * tile_width, tile_width, 1
        )
        update = jnp.einsum("rb,mb->rm", residual_tile, diag_inverse, precision=highest)
        iterate_rows = iterate_rows + update
    return (iterate_rows, residual)


def solution(mesh):
    placed = (
        P(None, "row"),
        P(None, ("row", "pan")),
        P("row", None, "pan", None),
        P("row", None, "pan", None),
        P(None, "row"),
        P(("row", "pan"), None),
        P(("row", "pan"), None),
    )
    return jax.shard_map(
        on_device,
        mesh=mesh,
        in_specs=placed,
        out_specs=(P(None, ("row", "pan")), P(None, ("row", "pan"))),
        check_vma=False,
    )
```

profile of v0, /device:TPU:1, one launch (start us, length us, event | category | flops | bytes accessed | tf_op | source)
XLA Modules:
  0.0 225.6 jit_solution(9807114171824869542)
XLA Ops:
  7.2 2.1 copy.33
  9.4 0.0 reduce-scatter.3.cloned.1.call-start
  9.4 0.1 iota_compare_fusion
  9.5 0.8 and_convert_fusion
  10.3 15.4 %all-gather.5.cloned.1.call-done = f32[256,1024]{0,1:T(8,128)} async-done(((f32[256,512]{0,1:T(8,128)}), f32[256,1024]{0,1:T(8,128)}) %all-gather.5.cloned.1.call-update) | async-done | bytes 1048592 | tf_op jit(solution)/shard_map/all_gather | solution.py:31
  25.7 12.3 %bitcast_multiply_fusion.1 = f32[128,2,8,256]{0,3,2,1:T(8,128)} fusion(f32[256,2,512,1]{0,2,3,1:T(8,128)} %bitcast.45, f32[2,128,8,512]{3,2,1,0:T(8,128)} %param.9, f32[128,2,8]{0,2,1:T(8,128)S(1)} %and_convert_fusion), kind=kOutput, calls=%fused_computation.5 | convolution fusion | flops 3221749760 | bytes 7348224 | tf_op jit(solution)/shard_map/cikb,rcb->ickr/dot_general | solution.py:33
  38.0 2.2 copy.36
  40.2 39.2 %all_to_all.36 = f32[128,2,8,256]{3,2,1,0:T(8,128)S(1)} all-to-all(f32[128,2,8,256]{3,2,1,0:T(8,128)S(1)} %copy.36), channel_id=1, replica_groups=mesh['row'=64,'pan'=2] {'row'}, dimensions={0} | all-to-all | bytes 4194304 | tf_op jit(solution)/shard_map/all_to_all | solution.py:35
  79.5 0.2 copy.37
  79.7 2.0 copy-done.5
  81.7 3.8 %convolution_bitcast_fusion.1 = f32[256,2,512]{2,0,1:T(8,128)S(1)} fusion(f32[2,128,8,256]{3,2,1,0:T(8,128)S(1)} %bitcast.46, f32[2,128,8,512]{3,2,1,0:T(8,128)S(1)} %copy-done.5), kind=kOutput, calls=%fused_computation.7 | convolution fusion | flops 3221225472 | bytes 7340032 | tf_op jit(solution)/shard_map/ickm,ickr->rim/dot_general | solution.py:36
  85.5 0.3 copy.38
  85.9 1.3 copy.39
  87.3 9.3 %reduce-scatter.3.cloned.1.call-done = f32[256,512]{1,0:T(8,128)} async-done(((f32[256,1024]{1,0:T(8,128)}), f32[256,512]{1,0:T(8,128)}) %reduce-scatter.3.cloned.1.call-update) | async-done | bytes 524304 | tf_op jit(solution)/shard_map/reduce_scatter | solution.py:40
  96.6 3.9 %fusion.8 = f32[256,512]{1,0:T(8,128)} fusion(f32[256,512]{1,0:T(8,128)} %reduce-scatter.3.cloned.1.call-done, f32[512,512]{1,0:T(8,128)S(1)} %copy-done, f32[256,1024]{0,1:T(8,128)S(1)} %copy-done.4, s32[]{:T(128)S(6)} %select_n.17, f32[256,1024]{1,0:T(8,128)} %param.7, s32[]{:T(128)S(6)} %select_n.15), kind=kOutput, calls=%fused_computation.12 | convolution fusion | flops 805568512 | bytes 3145736 | tf_op jit(solution)/shard_map/rb,mb->rm/dot_general | solution.py:39
  100.5 0.0 all-gather.9.cloned.1.call-start
  100.6 13.2 %all-gather.7.cloned.1.call-done = f32[256,1024]{1,0:T(8,128)} async-done(((f32[256,512]{1,0:T(8,128)}), f32[256,1024]{1,0:T(8,128)}) %all-gather.7.cloned.1.call-update) | async-done | bytes 1048592 | tf_op jit(solution)/shard_map/all_gather | solution.py:43
  113.7 3.1 %convolution_add_fusion.2 = f32[256,512]{1,0:T(8,128)} fusion(f32[256,512]{1,0:T(8,128)} %param.8, f32[512,512]{1,0:T(8,128)S(1)} %copy-done.2, f32[256,1024]{1,0:T(8,128)} %all-gather.7.cloned.1.call-done, s32[]{:T(128)S(6)} %select_n.17), kind=kOutput, calls=%fused_computation.10 | convolution fusion | flops 805437440 | bytes 2621444 | tf_op jit(solution)/shard_map/rb,mb->rm/dot_general | solution.py:47
  116.8 0.3 reduce-scatter.5.cloned.1.call-start
  117.1 13.0 %all-gather.9.cloned.1.call-done = f32[256,1024]{1,0:T(8,128)} async-done(((f32[256,512]{1,0:T(8,128)}), f32[256,1024]{1,0:T(8,128)}) %all-gather.9.cloned.1.call-update) | async-done | bytes 1048592 | tf_op jit(solution)/shard_map/all_gather | solution.py:31
  130.0 2.1 reshape.49
  132.1 9.3 %bitcast_multiply_fusion = f32[128,2,8,256]{0,3,2,1:T(8,128)} fusion(f32[2,128,8,512]{3,2,1,0:T(8,128)} %param.9, f32[256,2,512,1]{2,1,0,3:T(2,128)S(1)} %bitcast.44, f32[128,2,8]{0,2,1:T(8,128)S(1)} %and_convert_fusion), kind=kOutput, calls=%fused_computation.4 | convolution fusion | flops 3221749760 | bytes 7348224 | tf_op jit(solution)/shard_map/cikb,rcb->ickr/dot_general | solution.py:33
  141.4 2.2 copy.42
  143.7 39.2 %all_to_all.37 = f32[128,2,8,256]{3,2,1,0:T(8,128)S(1)} all-to-all(f32[128,2,8,256]{3,2,1,0:T(8,128)S(1)} %copy.42), channel_id=1, replica_groups=mesh['row'=64,'pan'=2] {'row'}, dimensions={0} | all-to-all | bytes 4194304 | tf_op jit(solution)/shard_map/all_to_all | solution.py:35
  182.9 0.2 copy.43
  183.1 2.0 copy-done.6
  185.1 3.8 %convolution_bitcast_fusion = f32[2,32,8,512]{3,2,1,0:T(8,128)S(1)} fusion(f32[2,128,8,256]{3,2,1,0:T(8,128)S(1)} %bitcast.47, f32[2,128,8,512]{3,2,1,0:T(8,128)S(1)} %copy-done.6), kind=kOutput, calls=%fused_computation.6 | convolution fusion | flops 3221225472 | bytes 7340032 | tf_op jit(solution)/shard_map/ickm,ickr->rim/dot_general | solution.py:36
  188.9 1.1 copy.53
  190.1 9.3 %reduce-scatter.5.cloned.1.call-done = f32[256,512]{1,0:T(8,128)} async-done(((f32[256,1024]{1,0:T(8,128)}), f32[256,512]{1,0:T(8,128)}) %reduce-scatter.5.cloned.1.call-update) | async-done | bytes 524304 | tf_op jit(solution)/shard_map/reduce_scatter | solution.py:40
  199.5 3.2 %fusion.9 = f32[256,512]{1,0:T(8,128)} fusion(f32[256,512]{1,0:T(8,128)} %reduce-scatter.5.cloned.1.call-done, f32[512,512]{1,0:T(8,128)S(1)} %copy-done, f32[256,1024]{1,0:T(8,128)} %all-gather.9.cloned.1.call-done, s32[]{:T(128)S(6)} %select_n.17, f32[256,1024]{1,0:T(8,128)} %param.7, s32[]{:T(128)S(6)} %select_n.15), kind=kOutput, calls=%fused_computation.13 | convolution fusion | flops 805568512 | bytes 3145736 | tf_op jit(solution)/shard_map/rb,mb->rm/dot_general | solution.py:39
  202.7 13.2 %all-gather.11.cloned.1.call-done = f32[256,1024]{1,0:T(8,128)} async-done(((f32[256,512]{1,0:T(8,128)}), f32[256,1024]{1,0:T(8,128)}) %all-gather.11.cloned.1.call-update) | async-done | bytes 1048592 | tf_op jit(solution)/shard_map/all_gather | solution.py:43
  215.9 2.9 %convolution_add_fusion = f32[256,512]{1,0:T(8,128)} fusion(f32[256,512]{1,0:T(8,128)S(1)} %copy-done.1, f32[512,512]{1,0:T(8,128)S(1)} %copy-done.3, f32[256,1024]{1,0:T(8,128)} %all-gather.11.cloned.1.call-done, s32[]{:T(128)S(6)} %select_n.17), kind=kOutput, calls=%fused_computation.8 | convolution fusion | flops 805437440 | bytes 2621444 | tf_op jit(solution)/shard_map/rb,mb->rm/dot_general | solution.py:47
  (23 shorter events, 0.3 us)
Async XLA Ops:
  7.2 89.5 %copy-start = (f32[512,512]{1,0:T(8,128)S(1)}, f32[512,512]{1,0:T(8,128)}, u32[]{:S(2)}) copy-start(f32[512,512]{1,0:T(8,128)} %param.12) | copy-start | bytes 3145732
  7.2 18.5 %all-gather.5.cloned.1.call-start = ((), (), s32[]{:S(2)}) async-start(), calls=%async_computation.4 | async-start | bytes 1572864 | tf_op jit(solution)/shard_map/all_gather | solution.py:31
  9.4 87.3 %reduce-scatter.3.cloned.1.call-start = ((), (), s32[]{:S(2)}) async-start(), calls=%async_computation.5 | async-start | bytes 1572864 | tf_op jit(solution)/shard_map/reduce_scatter | solution.py:40
  79.5 2.2 copy-start.5
  85.9 10.8 %copy-start.4 = (f32[256,1024]{0,1:T(8,128)S(1)}, f32[256,1024]{0,1:T(8,128)}, u32[]{:S(2)}) copy-start(f32[256,1024]{0,1:T(8,128)} %all-gather.5.cloned.1.call-done) | copy-start | bytes 3145732
  87.2 26.5 %copy-start.2 = (f32[512,512]{1,0:T(8,128)S(1)}, f32[512,512]{1,0:T(8,128)}, u32[]{:S(2)}) copy-start(f32[512,512]{1,0:T(8,128)} %param.13) | copy-start | bytes 3145732
  87.2 26.5 %all-gather.7.cloned.1.call-start = ((), (), s32[]{:S(2)}) async-start(), calls=%async_computation.6 | async-start | bytes 1572864 | tf_op jit(solution)/shard_map/all_gather | solution.py:43
  100.5 29.5 %all-gather.9.cloned.1.call-start = ((), (), s32[]{:S(2)}) async-start(), calls=%async_computation.7 | async-start | bytes 1572864 | tf_op jit(solution)/shard_map/all_gather | solution.py:31
  116.8 82.6 %reduce-scatter.5.cloned.1.call-start = ((), (), s32[]{:S(2)}) async-start(), calls=%async_computation.8 | async-start | bytes 1572864 | tf_op jit(solution)/shard_map/reduce_scatter | solution.py:40
  182.9 2.2 copy-start.6
  190.0 25.9 %copy-start.1 = (f32[256,512]{1,0:T(8,128)S(1)}, f32[256,512]{1,0:T(8,128)}, u32[]{:S(2)}) copy-start(f32[256,512]{1,0:T(8,128)} %convolution_add_fusion.2) | copy-start | bytes 1572868
  190.1 25.9 %copy-start.3 = (f32[512,512]{1,0:T(8,128)S(1)}, f32[512,512]{1,0:T(8,128)}, u32[]{:S(2)}) copy-start(f32[512,512]{1,0:T(8,128)} %param.13) | copy-start | bytes 3145732
  190.1 25.8 %all-gather.11.cloned.1.call-start = ((), (), s32[]{:S(2)}) async-start(), calls=%async_computation.9 | async-start | bytes 1572864 | tf_op jit(solution)/shard_map/all_gather | solution.py:43
Sparse Core Ops, SparseCore 0:
  10.2 15.3 all-gather.4
  87.3 9.2 reduce-scatter.2
  100.6 13.0 all-gather.6
  116.9 13.0 all-gather.8
  190.2 9.2 reduce-scatter.4
  202.8 13.0 all-gather.10
where the time goes:
time: 226 us
  blocking collectives  78.5 us (35%)
  waiting for transfers between devices  73.5 us (33%)
  matrix products  42.3 us (19%)
  local copies, waits for them, and re-layouts  15.8 us (7%)
  between operations  14.3 us (6%)
    all_to_all x2, blocking collectives, on_device(): lax.all_to_all(projected, 'row', split_axis=0, concat_axis=1, tiled=True)  78.5 us
    all_gather x2, waiting for transfers between devices, on_device(): guess_full = lax.all_gather(iterate_rows, 'pan', axis=1, tiled=True)  28.3 us
    all_gather x2, waiting for transfers between devices, on_device(): residual_full = lax.all_gather(residual, 'pan', axis=1, tiled=True)  26.4 us
    dot_general x2, matrix products, on_device(): jnp.einsum('cikb,rcb->ickr', v_factor, guess_tiles, precision=highest)  21.6 us
    reduce_scatter x2, waiting for transfers between devices, on_device(): lax.psum_scatter(low_rank, 'pan', scatter_dimension=1, tiled=True)  18.7 us
    dot_general x2, matrix products, on_device(): jnp.einsum('ickm,ickr->rim', u_factor, received, precision=highest)  7.64 us
    dot_general x2, matrix products, on_device(): jnp.einsum('rb,mb->rm', guess_tile, diag_block, precision=highest)  7.07 us
    unnamed x15, local copies, waits for them, and re-layouts  6.15 us
  transfers between devices with their start and end apart: 6, of which 6 were waited for; matrix products, arithmetic and copies ran while one was open for 0% of the time, Pallas kernels for 0%

commit v1 on v0

v1 whole, which is shorter than its diff:
```python
import jax
import jax.numpy as jnp
from jax import lax
from jax.experimental import pallas as pl
from jax.experimental.pallas import tpu as pltpu
from jax.sharding import PartitionSpec as P

MESH = pl.DeviceIdType.MESH
F32 = jnp.float32
BF16 = jnp.bfloat16
CHUNK = 128
MB = 512


def split(x):
    hi = x.astype(BF16)
    return hi, (x - hi.astype(F32)).astype(BF16)


def kernel(
    rhs_hbm, g_hbm, v_hbm, u_hbm, ranks, d_hbm, di_hbm, sol_hbm, res_hbm,
    gin, rin, vf, vh, vl, uf, uth, utl, df, dh, dl, dif, dih, dil,
    rhs, state, peer, dense, low, low_in, send, recv, wide, out_buf,
    load_sem, store_sem, send_sem, recv_sem, g_send, g_recv, l_send, l_recv,
):
    row = lax.axis_index("row")
    pan = lax.axis_index("pan")
    other = 1 - pan
    width = d_hbm.shape[0]
    z, y, x = row // 16, (row // 4) % 4, row % 4

    def shifted(a, b, c, sign):
        return (
            lax.rem(z + sign * (a + c) + 8, 4) * 16
            + lax.rem(y + sign * (a + b) + 8, 4) * 4
            + lax.rem(x + sign * a + 8, 4)
        )

    load_g = pltpu.make_async_copy(g_hbm, gin, load_sem.at[0])
    load_v = [
        pltpu.make_async_copy(v_hbm.at[c], vf.at[c], load_sem.at[1 + n])
        for n, c in enumerate((pan, other))
    ]
    load_u = pltpu.make_async_copy(u_hbm, uf, load_sem.at[3])
    load_d = pltpu.make_async_copy(d_hbm, df, load_sem.at[4])
    load_di = pltpu.make_async_copy(di_hbm, dif, load_sem.at[5])
    own_columns = pl.ds(pl.multiple_of(pan * width, width), width)
    load_r = pltpu.make_async_copy(rhs_hbm.at[:, own_columns], rin, load_sem.at[6])
    load_g.start()
    load_v[0].start()
    load_v[1].start()

    barrier = pltpu.get_barrier_semaphore()
    pl.semaphore_signal(barrier, inc=1, device_id=(row, other), device_id_type=MESH)

    def greet(n, carry):
        pl.semaphore_signal(
            barrier, inc=1, device_id=(lax.rem(row + n, 64), pan), device_id_type=MESH
        )
        return carry

    lax.fori_loop(1, 64, greet, 0)

    load_d.start()
    load_di.start()
    load_r.start()
    load_u.start()

    load_g.wait()
    for q in range(2):
        state[0, q] = gin[q * CHUNK:(q + 1) * CHUNK, :].T

    components = lax.broadcasted_iota(jnp.int32, (8, width), 0) + 8 * pan

    def prepare_v(c):
        def body(d, carry):
            tiles = []
            for e in range(2):
                i = 2 * d + e
                rank = jnp.where(i == 2 * row + c, 0, ranks[c, i])
                tiles.append(jnp.where(components < rank, vf[c, i], 0.0))
            hi, lo = split(jnp.concatenate(tiles, axis=0))
            rows = pl.ds(pl.multiple_of(16 * d, 16), 16)
            vh[c, rows, :] = hi
            vl[c, rows, :] = lo
            return carry

        lax.fori_loop(0, 64, body, 0, unroll=4)

    def product(ah, al, operand, start, size, depth):
        hi = operand[:, :CHUNK]
        both = jnp.dot(ah[start:start + size, :], operand[...], preferred_element_type=F32)
        return (
            both[:, :CHUNK] + both[:, CHUNK:]
            + jnp.dot(al[start:start + size, :], hi, preferred_element_type=F32)
        )

    def widen(target, value):
        hi, lo = split(value)
        target[:, :CHUNK] = hi
        target[:, CHUNK:] = lo

    def project(slot, c, value):
        operand = wide.at[pl.ds(0, width)]
        widen(operand, value)
        for start in range(0, 1024, MB):
            part = product(vh.at[c], vl.at[c], operand, start, MB, width)
            send[slot, start // 16:(start + MB) // 16, c] = part.reshape(MB // 16, 2, 8, CHUNK)

    def message(slot, n, target):
        return pltpu.make_async_remote_copy(
            src_ref=send.at[slot, target],
            dst_ref=recv.at[slot, n],
            send_sem=send_sem.at[slot],
            recv_sem=recv_sem.at[slot],
            device_id=(target, pan),
            device_id_type=MESH,
        )

    def all_messages(slot):
        return pltpu.make_async_remote_copy(
            src_ref=send.at[slot, pl.ds(1, 63)],
            dst_ref=recv.at[slot, pl.ds(1, 63)],
            send_sem=send_sem.at[slot],
            recv_sem=recv_sem.at[slot],
            device_id=(row, other),
            device_id_type=MESH,
        )

    def scatter(slot):
        for a in range(1, 4):
            message(slot, a, shifted(a, 0, 0, 1)).start()

        def body(m, carry):
            b, c = m % 4, m // 4
            for a in range(4):
                message(slot, 4 * m + a, shifted(a, b, c, 1)).start()
            return carry

        lax.fori_loop(1, 16, body, 0)
        recv[slot, 0] = send[slot, row]

    def to_peer(source, target, sems, recvs, n):
        return pltpu.make_async_remote_copy(
            src_ref=source,
            dst_ref=target,
            send_sem=sems.at[n],
            recv_sem=recvs.at[n],
            device_id=(row, other),
            device_id_type=MESH,
        )

    def guess_copy(it, q):
        return to_peer(state.at[it, q], peer.at[it, q], g_send, g_recv, 2 * it + q)

    def low_copy(slot):
        return to_peer(low.at[slot], low_in.at[slot], l_send, l_recv, slot)

    load_v[0].wait()
    prepare_v(pan)
    pl.semaphore_wait(barrier, 64)
    for q in range(2):
        guess_copy(0, q).start()
    project(0, pan, state[0, 0])
    load_v[1].wait()
    prepare_v(other)
    guess_copy(0, 0).wait_recv()
    project(0, other, peer[0, 0])
    scatter(0)
    project(1, pan, state[0, 1])
    guess_copy(0, 1).wait_recv()
    project(1, other, peer[0, 1])
    scatter(1)

    load_u.wait()
    for i in range(2):
        def turn(m, carry):
            pieces = []
            for n in range(8):
                order = 8 * m + n
                a, b, c = order % 4, (order // 4) % 4, order // 16
                source = shifted(a, b, c, -1)
                for e in range(2):
                    pieces.append(uf[i, 2 * source + e])
            hi, lo = split(jnp.concatenate(pieces, axis=0).T)
            columns = pl.ds(pl.multiple_of(128 * m, 128), 128)
            uth[i, :, columns] = hi
            utl[i, :, columns] = lo
            return carry

        lax.fori_loop(0, 8, turn, 0)
    load_d.wait()
    dh[...], dl[...] = split(df[...])
    load_di.wait()
    dih[...], dil[...] = split(dif[...])
    load_r.wait()

    def subtract_dense(it, q):
        operand = wide.at[pl.ds(0, width)]
        widen(operand, state[it, q])
        dense[q] = rhs[q] - product(dh, dl, operand, 0, width, width)

    for q in range(2):
        rhs[q] = rin[q * CHUNK:(q + 1) * CHUNK, :].T
        subtract_dense(0, q)

    def low_rank(slot, i):
        widen(wide, recv[slot, :, :, i].reshape(1024, CHUNK))
        return product(uth.at[i], utl.at[i], wide, 0, width, 1024)

    def advance(it, q):
        slot = 2 * it + q
        all_messages(slot).wait_recv()
        low[slot] = low_rank(slot, other)
        low_copy(slot).start()
        own = low_rank(slot, pan)
        low_copy(slot).wait_recv()
        residual = dense[q] - (own + low_in[slot])
        operand = wide.at[pl.ds(0, width)]
        widen(operand, residual)
        update = product(dih, dil, operand, 0, width, width)
        return residual, state[it, q] + update

    for q in range(2):
        residual, guess = advance(0, q)
        state[1, q] = guess
        guess_copy(1, q).start()
        project(2 + q, pan, guess)
        guess_copy(1, q).wait_recv()
        project(2 + q, other, peer[1, q])
        scatter(2 + q)
        subtract_dense(1, q)

    stores = []
    for q in range(2):
        residual, guess = advance(1, q)
        out_buf[0, q] = residual.T
        out_buf[1, q] = guess.T
        for n, target in enumerate((res_hbm, sol_hbm)):
            store = pltpu.make_async_copy(
                out_buf.at[n, q], target.at[pl.ds(q * CHUNK, CHUNK)], store_sem.at[2 * n + q]
            )
            store.start()
            stores.append(store)

    for slot in range(4):
        all_messages(slot).wait_send()
        low_copy(slot).wait_send()
        guess_copy(slot // 2, slot % 2).wait_send()
    for store in stores:
        store.wait()


def on_device(right_side, initial_guess, v_factor, u_factor, tile_ranks, diag_block, diag_inverse):
    any_space = pl.BlockSpec(memory_space=pl.ANY)
    tiles, count, part, width = v_factor.shape
    rhs_count = initial_guess.shape[0]
    shape = jax.ShapeDtypeStruct(initial_guess.shape, F32)
    sol, res = pl.pallas_call(
        kernel,
        name="richardson",
        out_shape=(shape, shape),
        in_specs=[any_space] * 4 + [pl.BlockSpec(memory_space=pltpu.SMEM)] + [any_space] * 2,
        out_specs=(any_space, any_space),
        scratch_shapes=[
            pltpu.VMEM((rhs_count, width), F32),
            pltpu.VMEM((rhs_count, width), F32),
            pltpu.VMEM((tiles, count, part, width), F32),
            pltpu.VMEM((tiles, count * part, width), BF16),
            pltpu.VMEM((tiles, count * part, width), BF16),
            pltpu.VMEM((tiles, count, part, width), F32),
            pltpu.VMEM((tiles, width, count * part), BF16),
            pltpu.VMEM((tiles, width, count * part), BF16),
            pltpu.VMEM((width, width), F32),
            pltpu.VMEM((width, width), BF16),
            pltpu.VMEM((width, width), BF16),
            pltpu.VMEM((width, width), F32),
            pltpu.VMEM((width, width), BF16),
            pltpu.VMEM((width, width), BF16),
            pltpu.VMEM((2, width, CHUNK), F32),
            pltpu.VMEM((2, 2, width, CHUNK), F32),
            pltpu.VMEM((2, 2, width, CHUNK), F32),
            pltpu.VMEM((2, width, CHUNK), F32),
            pltpu.VMEM((4, width, CHUNK), F32),
            pltpu.VMEM((4, width, CHUNK), F32),
            pltpu.VMEM((4, 64, tiles, tiles, part, CHUNK), F32),
            pltpu.VMEM((4, 64, tiles, tiles, part, CHUNK), F32),
            pltpu.VMEM((1024, 2 * CHUNK), BF16),
            pltpu.VMEM((2, 2, CHUNK, width), F32),
            pltpu.SemaphoreType.DMA((7,)),
            pltpu.SemaphoreType.DMA((4,)),
            pltpu.SemaphoreType.DMA((4,)),
            pltpu.SemaphoreType.DMA((4,)),
            pltpu.SemaphoreType.DMA((4,)),
            pltpu.SemaphoreType.DMA((4,)),
            pltpu.SemaphoreType.DMA((4,)),
            pltpu.SemaphoreType.DMA((4,)),
        ],
        compiler_params=pltpu.CompilerParams(
            collective_id=0, has_side_effects=True, vmem_limit_bytes=56 << 20
        ),
    )(right_side, initial_guess, v_factor, u_factor, tile_ranks.T, diag_block, diag_inverse)
    return sol, res


def solution(mesh):
    placed = (
        P(None, "row"),
        P(None, ("row", "pan")),
        P("row", None, "pan", None),
        P("row", None, "pan", None),
        P(None, "row"),
        P(("row", "pan"), None),
        P(("row", "pan"), None),
    )
    return jax.shard_map(
        on_device,
        mesh=mesh,
        in_specs=placed,
        out_specs=(P(None, ("row", "pan")), P(None, ("row", "pan"))),
        check_vma=False,
    )
```

time: 226 us -> 79.5 us (0.35)
  the two profiles are of different devices: /device:TPU:1 before, /device:TPU:35 now
where the time goes in v1:
time: 79.5 us; the launch traced here: 79.3 us
  Pallas kernels  74.9 us (94%)
  local copies, waits for them, and re-layouts  3.74 us (5%)
    pallas_call x1, Pallas kernels, on_device(): pl.pallas_call(kernel, name='richardson', out_shape=(shape, shape), in_sp...  74.9 us
    unnamed x2, local copies, waits for them, and re-layouts  3.74 us

profile of v1, /device:TPU:35, one launch (start us, length us, event | category | flops | bytes accessed | tf_op | source)
XLA Modules:
  0.0 79.3 jit_solution(6284828078837964167)
XLA Ops:
  0.6 74.9 %richardson.1 = (f32[256,512]{1,0:T(8,128)}, f32[256,512]{1,0:T(8,128)}) custom-call(f32[256,1024]{1,0:T(8,128)} %rhs_hbm.1, f32[256,512]{1,0:T(8,128)} %g_hbm.1, f32[2,128,8,512]{3,2,1,0:T(8,128)} %v_hbm.1, f32[2,128,8,512]{3,2,1,0:T(8,128)} %u_hbm.1, s32[2,128]{1,0:T(2,128)} %bitcast.1, f32[512,512]{1,0:T(8,128)} %d_hbm.1, f32[512,512]{1,0:T(8,128)} %di_hbm.1), custom_call_target="tpu_custom_call" | custom-call | tf_op jit(solution)/shard_map/richardson/pallas_call | solution.py:259
  75.5 1.9 %copy.11 = f32[256,512]{1,0:T(8,128)} copy(f32[256,512]{1,0:T(8,128)} %get-tuple-element.4) | data formatting | bytes 1048576
  77.4 1.9 %copy.12 = f32[256,512]{1,0:T(8,128)} copy(f32[256,512]{1,0:T(8,128)} %get-tuple-element.5) | data formatting | bytes 1048576

commit v2 on v1

--- a/solution.py
+++ b/solution.py
@@ -18,10 +18,10 @@
 
 
 def kernel(
-    rhs_hbm, g_hbm, v_hbm, u_hbm, ranks, d_hbm, di_hbm, sol_hbm, res_hbm,
+    rhs_hbm, g_hbm, v_hbm, u_hbm, ranks, d_hbm, di_hbm, result,
     gin, rin, vf, vh, vl, uf, uth, utl, df, dh, dl, dif, dih, dil,
-    rhs, state, peer, dense, low, low_in, send, recv, wide, out_buf,
-    load_sem, store_sem, send_sem, recv_sem, g_send, g_recv, l_send, l_recv,
+    rhs, state, peer, dense, low, low_in, send, recv, wide,
+    load_sem, send_sem, recv_sem, g_send, g_recv, l_send, l_recv,
 ):
     row = lax.axis_index("row")
     pan = lax.axis_index("pan")
@@ -31,8 +31,8 @@
 
     def shifted(a, b, c, sign):
         return (
-            lax.rem(z + sign * (a + c) + 8, 4) * 16
-            + lax.rem(y + sign * (a + b) + 8, 4) * 4
+            lax.rem(z - sign * (a + b) + 8, 4) * 16
+            + lax.rem(y + sign * (a + 2 * b + c) + 16, 4) * 4
             + lax.rem(x + sign * a + 8, 4)
         )
 
@@ -72,20 +72,16 @@
 
     components = lax.broadcasted_iota(jnp.int32, (8, width), 0) + 8 * pan
 
-    def prepare_v(c):
-        def body(d, carry):
-            tiles = []
-            for e in range(2):
-                i = 2 * d + e
-                rank = jnp.where(i == 2 * row + c, 0, ranks[c, i])
-                tiles.append(jnp.where(components < rank, vf[c, i], 0.0))
-            hi, lo = split(jnp.concatenate(tiles, axis=0))
-            rows = pl.ds(pl.multiple_of(16 * d, 16), 16)
-            vh[c, rows, :] = hi
-            vl[c, rows, :] = lo
-            return carry
-
-        lax.fori_loop(0, 64, body, 0, unroll=4)
+    def prepare_v(c, d):
+        tiles = []
+        for e in range(2):
+            i = 2 * d + e
+            rank = jnp.where(i == 2 * row + c, 0, ranks[c, i])
+            tiles.append(jnp.where(components < rank, vf[c, i], 0.0))
+        hi, lo = split(jnp.concatenate(tiles, axis=0))
+        rows = pl.ds(pl.multiple_of(16 * d, 16), 16)
+        vh[c, rows, :] = hi
+        vl[c, rows, :] = lo
 
     def product(ah, al, operand, start, size, depth):
         hi = operand[:, :CHUNK]
@@ -127,18 +123,45 @@
             device_id_type=MESH,
         )
 
-    def scatter(slot):
-        for a in range(1, 4):
-            message(slot, a, shifted(a, 0, 0, 1)).start()
+    def half_message(slot, n, target, c):
+        return pltpu.make_async_remote_copy(
+            src_ref=send.at[slot, target, c],
+            dst_ref=recv.at[slot, n, c],
+            send_sem=send_sem.at[slot],
+            recv_sem=recv_sem.at[slot],
+            device_id=(target, pan),
+            device_id_type=MESH,
+        )
+
+    def in_order(visit):
+        for a in range(4):
+            visit(a, a, 0, 0)
 
         def body(m, carry):
             b, c = m % 4, m // 4
             for a in range(4):
-                message(slot, 4 * m + a, shifted(a, b, c, 1)).start()
+                visit(4 * m + a, a, b, c)
             return carry
 
         lax.fori_loop(1, 16, body, 0)
+
+    def scatter(slot):
+        def visit(n, a, b, c):
+            if not (isinstance(n, int) and n == 0):
+                message(slot, n, shifted(a, b, c, 1)).start()
+
+        in_order(visit)
         recv[slot, 0] = send[slot, row]
+
+    def scatter_half(slot, part, beside=None):
+        def visit(n, a, b, c):
+            if not (isinstance(n, int) and n == 0):
+                half_message(slot, n, shifted(a, b, c, 1), part).start()
+            if beside is not None:
+                beside(n)
+
+        in_order(visit)
+        recv[slot, 0, part] = send[slot, row, part]
 
     def to_peer(source, target, sems, recvs, n):
         return pltpu.make_async_remote_copy(
@@ -157,16 +180,21 @@
         return to_peer(low.at[slot], low_in.at[slot], l_send, l_recv, slot)
 
     load_v[0].wait()
-    prepare_v(pan)
+
+    def prepare_own(d, carry):
+        prepare_v(pan, d)
+        return carry
+
+    lax.fori_loop(0, 64, prepare_own, 0, unroll=4)
+    project(0, pan, state[0, 0])
     pl.semaphore_wait(barrier, 64)
     for q in range(2):
         guess_copy(0, q).start()
-    project(0, pan, state[0, 0])
     load_v[1].wait()
-    prepare_v(other)
+    scatter_half(0, pan, lambda d: prepare_v(other, d))
     guess_copy(0, 0).wait_recv()
     project(0, other, peer[0, 0])
-    scatter(0)
+    scatter_half(0, other)
     project(1, pan, state[0, 1])
     guess_copy(0, 1).wait_recv()
     project(1, other, peer[0, 1])
@@ -231,22 +259,26 @@
         scatter(2 + q)
         subtract_dense(1, q)
 
+    for q in range(2):
+        residual, guess = advance(1, q)
+        result[0, q] = guess
+        result[1, q] = residual
+
+    for slot in range(4):
+        all_messages(slot).wait_send()
+        low_copy(slot).wait_send()
+        guess_copy(slot // 2, slot % 2).wait_send()
+
+def finish(result, sol_hbm, res_hbm, out_buf, store_sem):
     stores = []
     for q in range(2):
-        residual, guess = advance(1, q)
-        out_buf[0, q] = residual.T
-        out_buf[1, q] = guess.T
-        for n, target in enumerate((res_hbm, sol_hbm)):
+        for n, target in enumerate((sol_hbm, res_hbm)):
+            out_buf[n, q] = result[n, q].T
             store = pltpu.make_async_copy(
                 out_buf.at[n, q], target.at[pl.ds(q * CHUNK, CHUNK)], store_sem.at[2 * n + q]
             )
             store.start()
             stores.append(store)
-
-    for slot in range(4):
-        all_messages(slot).wait_send()
-        low_copy(slot).wait_send()
-        guess_copy(slot // 2, slot % 2).wait_send()
     for store in stores:
         store.wait()
 
@@ -256,12 +288,12 @@
     tiles, count, part, width = v_factor.shape
     rhs_count = initial_guess.shape[0]
     shape = jax.ShapeDtypeStruct(initial_guess.shape, F32)
-    sol, res = pl.pallas_call(
+    result = pl.pallas_call(
         kernel,
         name="richardson",
-        out_shape=(shape, shape),
+        out_shape=pltpu.VMEM((2, 2, width, CHUNK), F32),
         in_specs=[any_space] * 4 + [pl.BlockSpec(memory_space=pltpu.SMEM)] + [any_space] * 2,
-        out_specs=(any_space, any_space),
+        out_specs=pl.BlockSpec(memory_space=pltpu.VMEM),
         scratch_shapes=[
             pltpu.VMEM((rhs_count, width), F32),
             pltpu.VMEM((rhs_count, width), F32),
@@ -286,9 +318,7 @@
             pltpu.VMEM((4, 64, tiles, tiles, part, CHUNK), F32),
             pltpu.VMEM((4, 64, tiles, tiles, part, CHUNK), F32),
             pltpu.VMEM((1024, 2 * CHUNK), BF16),
-            pltpu.VMEM((2, 2, CHUNK, width), F32),
             pltpu.SemaphoreType.DMA((7,)),
-            pltpu.SemaphoreType.DMA((4,)),
             pltpu.SemaphoreType.DMA((4,)),
             pltpu.SemaphoreType.DMA((4,)),
             pltpu.SemaphoreType.DMA((4,)),
@@ -297,10 +327,21 @@
             pltpu.SemaphoreType.DMA((4,)),
         ],
         compiler_params=pltpu.CompilerParams(
-            collective_id=0, has_side_effects=True, vmem_limit_bytes=56 << 20
+            collective_id=0, has_side_effects=True, vmem_limit_bytes=58 << 20
         ),
     )(right_side, initial_guess, v_factor, u_factor, tile_ranks.T, diag_block, diag_inverse)
-    return sol, res
+    return pl.pallas_call(
+        finish,
+        name="finish",
+        out_shape=(shape, shape),
+        in_specs=[pl.BlockSpec(memory_space=pltpu.VMEM)],
+        out_specs=(any_space, any_space),
+        scratch_shapes=[
+            pltpu.VMEM((2, 2, CHUNK, width), F32),
+            pltpu.SemaphoreType.DMA((4,)),
+        ],
+        compiler_params=pltpu.CompilerParams(vmem_limit_bytes=8 << 20),
+    )(result)
 
 
 def solution(mesh):

time: 79.5 us -> 64 us (0.81)
  the two profiles are of different devices: /device:TPU:35 before, /device:TPU:1 now
where the time goes in v2:
time: 64 us; the launch traced here: 63.9 us
  Pallas kernels  63.1 us (99%)
  between operations  0.8 us (1%)
    pallas_call x1, Pallas kernels, on_device(): pl.pallas_call(kernel, name='richardson', out_shape=pltpu.VMEM((2, 2, wid...  62 us

profile of v2, /device:TPU:1, one launch (start us, length us, event | category | flops | bytes accessed | tf_op | source)
XLA Modules:
  0.0 63.9 jit_solution(13307661306429171774)
XLA Ops:
  0.6 62.0 %richardson.1.result = f32[2,2,512,128]{3,2,1,0:T(8,128)S(1)} custom-call(f32[256,1024]{1,0:T(8,128)} %rhs_hbm.1, f32[256,512]{1,0:T(8,128)} %g_hbm.1, f32[2,128,8,512]{3,2,1,0:T(8,128)} %v_hbm.1, f32[2,128,8,512]{3,2,1,0:T(8,128)} %u_hbm.1, s32[2,128]{1,0:T(2,128)} %bitcast.1, f32[512,512]{1,0:T(8,128)} %d_hbm.1, f32[512,512]{1,0:T(8,128)} %di_hbm.1), custom_call_target="tpu_custom_call" | custom-call | tf_op jit(solution)/shard_map/richardson/pallas_call | solution.py:291
  62.6 1.1 %finish.1 = (f32[256,512]{1,0:T(8,128)}, f32[256,512]{1,0:T(8,128)}) custom-call(f32[2,2,512,128]{3,2,1,0:T(8,128)S(1)} %richardson.1.result), custom_call_target="tpu_custom_call" | custom-call | tf_op jit(solution)/shard_map/finish/pallas_call | solution.py:333

commit v3 on v2

--- a/solution.py
+++ b/solution.py
@@ -9,7 +9,11 @@
 F32 = jnp.float32
 BF16 = jnp.bfloat16
 CHUNK = 128
-MB = 512
+MB = 1024
+EARLY = 40
+
+
+SHIFTS = [(-(a + b) % 4, (a + 2 * b + c) % 4, a) for c in range(4) for b in range(4) for a in range(4)]
 
 
 def split(x):
@@ -18,10 +22,10 @@
 
 
 def kernel(
-    rhs_hbm, g_hbm, v_hbm, u_hbm, ranks, d_hbm, di_hbm, result,
+    rhs_hbm, g_hbm, v_hbm, u_hbm, ranks_hbm, d_hbm, di_hbm, result,
     gin, rin, vf, vh, vl, uf, uth, utl, df, dh, dl, dif, dih, dil,
-    rhs, state, peer, dense, low, low_in, send, recv, wide,
-    load_sem, send_sem, recv_sem, g_send, g_recv, l_send, l_recv,
+    rhs, state, peer, dense, low, low_in, part, send, recv, wide,
+    ranks, targets, sources, load_sem, send_sem, recv_sem, g_send, g_recv, l_send, l_recv,
 ):
     row = lax.axis_index("row")
     pan = lax.axis_index("pan")
@@ -29,11 +33,12 @@
     width = d_hbm.shape[0]
     z, y, x = row // 16, (row // 4) % 4, row % 4
 
-    def shifted(a, b, c, sign):
+    def shifted(n, sign):
+        dz, dy, dx = SHIFTS[n]
         return (
-            lax.rem(z - sign * (a + b) + 8, 4) * 16
-            + lax.rem(y + sign * (a + 2 * b + c) + 16, 4) * 4
-            + lax.rem(x + sign * a + 8, 4)
+            lax.rem(z + sign * dz + 4, 4) * 16
+            + lax.rem(y + sign * dy + 4, 4) * 4
+            + lax.rem(x + sign * dx + 4, 4)
         )
 
     load_g = pltpu.make_async_copy(g_hbm, gin, load_sem.at[0])
@@ -46,9 +51,9 @@
     load_di = pltpu.make_async_copy(di_hbm, dif, load_sem.at[5])
     own_columns = pl.ds(pl.multiple_of(pan * width, width), width)
     load_r = pltpu.make_async_copy(rhs_hbm.at[:, own_columns], rin, load_sem.at[6])
+    load_ranks = pltpu.make_async_copy(ranks_hbm, ranks, load_sem.at[7])
     load_g.start()
     load_v[0].start()
-    load_v[1].start()
 
     barrier = pltpu.get_barrier_semaphore()
     pl.semaphore_signal(barrier, inc=1, device_id=(row, other), device_id_type=MESH)
@@ -59,12 +64,11 @@
         )
         return carry
 
-    lax.fori_loop(1, 64, greet, 0)
-
-    load_d.start()
-    load_di.start()
-    load_r.start()
-    load_u.start()
+    lax.fori_loop(1, 64, greet, 0, unroll=9)
+    load_ranks.start()
+    load_v[1].start()
+    for n in range(1, 64):
+        targets[n] = shifted(n, 1)
 
     load_g.wait()
     for q in range(2):
@@ -83,12 +87,11 @@
         vh[c, rows, :] = hi
         vl[c, rows, :] = lo
 
-    def product(ah, al, operand, start, size, depth):
-        hi = operand[:, :CHUNK]
-        both = jnp.dot(ah[start:start + size, :], operand[...], preferred_element_type=F32)
+    def product(ah, al, operand):
+        both = jnp.dot(ah[...], operand[...], preferred_element_type=F32)
         return (
             both[:, :CHUNK] + both[:, CHUNK:]
-            + jnp.dot(al[start:start + size, :], hi, preferred_element_type=F32)
+            + jnp.dot(al[...], operand[:, :CHUNK], preferred_element_type=F32)
         )
 
     def widen(target, value):
@@ -100,25 +103,27 @@
         operand = wide.at[pl.ds(0, width)]
         widen(operand, value)
         for start in range(0, 1024, MB):
-            part = product(vh.at[c], vl.at[c], operand, start, MB, width)
-            send[slot, start // 16:(start + MB) // 16, c] = part.reshape(MB // 16, 2, 8, CHUNK)
+            rows = pl.ds(start, MB)
+            block = product(vh.at[c, rows], vl.at[c, rows], operand)
+            send[slot, start // 16:(start + MB) // 16, c] = block.reshape(MB // 16, 2, 8, CHUNK)
 
     def message(slot, n, target):
         return pltpu.make_async_remote_copy(
             src_ref=send.at[slot, target],
             dst_ref=recv.at[slot, n],
             send_sem=send_sem.at[slot],
-            recv_sem=recv_sem.at[slot],
+            recv_sem=recv_sem.at[slot, n // EARLY],
             device_id=(target, pan),
             device_id_type=MESH,
         )
 
-    def all_messages(slot):
+    def all_messages(slot, late):
+        first, count = (EARLY, 64 - EARLY) if late else (1, EARLY - 1)
         return pltpu.make_async_remote_copy(
-            src_ref=send.at[slot, pl.ds(1, 63)],
-            dst_ref=recv.at[slot, pl.ds(1, 63)],
+            src_ref=send.at[slot, pl.ds(first, count)],
+            dst_ref=recv.at[slot, pl.ds(first, count)],
             send_sem=send_sem.at[slot],
-            recv_sem=recv_sem.at[slot],
+            recv_sem=recv_sem.at[slot, late],
             device_id=(row, other),
             device_id_type=MESH,
         )
@@ -128,40 +133,36 @@
             src_ref=send.at[slot, target, c],
             dst_ref=recv.at[slot, n, c],
             send_sem=send_sem.at[slot],
-            recv_sem=recv_sem.at[slot],
+            recv_sem=recv_sem.at[slot, n // EARLY],
             device_id=(target, pan),
             device_id_type=MESH,
         )
 
     def in_order(visit):
-        for a in range(4):
-            visit(a, a, 0, 0)
+        for n in range(1, 4):
+            visit(n)
 
         def body(m, carry):
-            b, c = m % 4, m // 4
-            for a in range(4):
-                visit(4 * m + a, a, b, c)
+            for n in range(4):
+                visit(4 * m + n)
             return carry
 
         lax.fori_loop(1, 16, body, 0)
 
     def scatter(slot):
-        def visit(n, a, b, c):
-            if not (isinstance(n, int) and n == 0):
-                message(slot, n, shifted(a, b, c, 1)).start()
-
-        in_order(visit)
+        in_order(lambda n: message(slot, n, targets[n]).start())
         recv[slot, 0] = send[slot, row]
 
-    def scatter_half(slot, part, beside=None):
-        def visit(n, a, b, c):
-            if not (isinstance(n, int) and n == 0):
-                half_message(slot, n, shifted(a, b, c, 1), part).start()
+    def scatter_half(slot, tile, beside=None):
+        def visit(n):
+            half_message(slot, n, targets[n], tile).start()
             if beside is not None:
                 beside(n)
 
+        if beside is not None:
+            beside(0)
         in_order(visit)
-        recv[slot, 0, part] = send[slot, row, part]
+        recv[slot, 0, tile] = send[slot, row, tile]
 
     def to_peer(source, target, sems, recvs, n):
         return pltpu.make_async_remote_copy(
@@ -180,6 +181,7 @@
         return to_peer(low.at[slot], low_in.at[slot], l_send, l_recv, slot)
 
     load_v[0].wait()
+    load_ranks.wait()
 
     def prepare_own(d, carry):
         prepare_v(pan, d)
@@ -191,6 +193,8 @@
     for q in range(2):
         guess_copy(0, q).start()
     load_v[1].wait()
+    for load in (load_d, load_di, load_r, load_u):
+        load.start()
     scatter_half(0, pan, lambda d: prepare_v(other, d))
     guess_copy(0, 0).wait_recv()
     project(0, other, peer[0, 0])
@@ -200,14 +204,14 @@
     project(1, other, peer[0, 1])
     scatter(1)
 
+    for n in range(64):
+        sources[n] = shifted(n, -1)
     load_u.wait()
     for i in range(2):
         def turn(m, carry):
             pieces = []
             for n in range(8):
-                order = 8 * m + n
-                a, b, c = order % 4, (order // 4) % 4, order // 16
-                source = shifted(a, b, c, -1)
+                source = sources[8 * m + n]
                 for e in range(2):
                     pieces.append(uf[i, 2 * source + e])
             hi, lo = split(jnp.concatenate(pieces, axis=0).T)
@@ -226,28 +230,33 @@
     def subtract_dense(it, q):
         operand = wide.at[pl.ds(0, width)]
         widen(operand, state[it, q])
-        dense[q] = rhs[q] - product(dh, dl, operand, 0, width, width)
+        dense[q] = rhs[q] - product(dh, dl, operand)
 
     for q in range(2):
         rhs[q] = rin[q * CHUNK:(q + 1) * CHUNK, :].T
         subtract_dense(0, q)
 
-    def low_rank(slot, i):
-        widen(wide, recv[slot, :, :, i].reshape(1024, CHUNK))
-        return product(uth.at[i], utl.at[i], wide, 0, width, 1024)
+    def low_rank(slot, i, late):
+        first, count = (EARLY, 64 - EARLY) if late else (0, EARLY)
+        columns = pl.ds(16 * first, 16 * count)
+        operand = wide.at[columns]
+        widen(operand, recv[slot, first:first + count, :, i].reshape(16 * count, CHUNK))
+        return product(uth.at[i, :, columns], utl.at[i, :, columns], operand)
 
     def advance(it, q):
         slot = 2 * it + q
-        all_messages(slot).wait_recv()
-        low[slot] = low_rank(slot, other)
+        all_messages(slot, 0).wait_recv()
+        part[0] = low_rank(slot, other, 0)
+        part[1] = low_rank(slot, pan, 0)
+        all_messages(slot, 1).wait_recv()
+        low[slot] = part[0] + low_rank(slot, other, 1)
         low_copy(slot).start()
-        own = low_rank(slot, pan)
+        own = dense[q] - (part[1] + low_rank(slot, pan, 1))
         low_copy(slot).wait_recv()
-        residual = dense[q] - (own + low_in[slot])
+        residual = own - low_in[slot]
         operand = wide.at[pl.ds(0, width)]
         widen(operand, residual)
-        update = product(dih, dil, operand, 0, width, width)
-        return residual, state[it, q] + update
+        return residual, state[it, q] + product(dih, dil, operand)
 
     for q in range(2):
         residual, guess = advance(0, q)
@@ -261,24 +270,22 @@
 
     for q in range(2):
         residual, guess = advance(1, q)
-        result[0, q] = guess
-        result[1, q] = residual
+        result[0, q * CHUNK:(q + 1) * CHUNK] = guess.T
+        result[1, q * CHUNK:(q + 1) * CHUNK] = residual.T
 
     for slot in range(4):
-        all_messages(slot).wait_send()
+        for late in range(2):
+            all_messages(slot, late).wait_send()
         low_copy(slot).wait_send()
         guess_copy(slot // 2, slot % 2).wait_send()
 
-def finish(result, sol_hbm, res_hbm, out_buf, store_sem):
-    stores = []
-    for q in range(2):
-        for n, target in enumerate((sol_hbm, res_hbm)):
-            out_buf[n, q] = result[n, q].T
-            store = pltpu.make_async_copy(
-                out_buf.at[n, q], target.at[pl.ds(q * CHUNK, CHUNK)], store_sem.at[2 * n + q]
-            )
-            store.start()
-            stores.append(store)
+def finish(result, sol_hbm, res_hbm, store_sem):
+    stores = [
+        pltpu.make_async_copy(result.at[n], target, store_sem.at[n])
+        for n, target in enumerate((sol_hbm, res_hbm))
+    ]
+    for store in stores:
+        store.start()
     for store in stores:
         store.wait()
 
@@ -291,8 +298,8 @@
     result = pl.pallas_call(
         kernel,
         name="richardson",
-        out_shape=pltpu.VMEM((2, 2, width, CHUNK), F32),
-        in_specs=[any_space] * 4 + [pl.BlockSpec(memory_space=pltpu.SMEM)] + [any_space] * 2,
+        out_shape=pltpu.VMEM((2, rhs_count, width), F32),
+        in_specs=[any_space] * 7,
         out_specs=pl.BlockSpec(memory_space=pltpu.VMEM),
         scratch_shapes=[
             pltpu.VMEM((rhs_count, width), F32),
@@ -315,12 +322,16 @@
             pltpu.VMEM((2, width, CHUNK), F32),
             pltpu.VMEM((4, width, CHUNK), F32),
             pltpu.VMEM((4, width, CHUNK), F32),
+            pltpu.VMEM((2, width, CHUNK), F32),
             pltpu.VMEM((4, 64, tiles, tiles, part, CHUNK), F32),
             pltpu.VMEM((4, 64, tiles, tiles, part, CHUNK), F32),
             pltpu.VMEM((1024, 2 * CHUNK), BF16),
-            pltpu.SemaphoreType.DMA((7,)),
-            pltpu.SemaphoreType.DMA((4,)),
-            pltpu.SemaphoreType.DMA((4,)),
+            pltpu.SMEM(tile_ranks.shape[::-1], jnp.int32),
+            pltpu.SMEM((64,), jnp.int32),
+            pltpu.SMEM((64,), jnp.int32),
+            pltpu.SemaphoreType.DMA((8,)),
+            pltpu.SemaphoreType.DMA((4,)),
+            pltpu.SemaphoreType.DMA((4, 2)),
             pltpu.SemaphoreType.DMA((4,)),
             pltpu.SemaphoreType.DMA((4,)),
             pltpu.SemaphoreType.DMA((4,)),
@@ -336,10 +347,7 @@
         out_shape=(shape, shape),
         in_specs=[pl.BlockSpec(memory_space=pltpu.VMEM)],
         out_specs=(any_space, any_space),
-        scratch_shapes=[
-            pltpu.VMEM((2, 2, CHUNK, width), F32),
-            pltpu.SemaphoreType.DMA((4,)),
-        ],
+        scratch_shapes=[pltpu.SemaphoreType.DMA((2,))],
         compiler_params=pltpu.CompilerParams(vmem_limit_bytes=8 << 20),
     )(result)
 

time: 64 us -> 62.9 us (0.983)
  Pallas kernels: 63.1 us -> 62 us
    pallas_call x1, Pallas kernels: 62 us -> 61 us  [on_device(): pl.pallas_call(kernel, name='richardson', out_shape=pltpu.VMEM((2, rhs_co...]
where the time goes in v3:
time: 62.9 us; the launch traced here: 62.8 us
  Pallas kernels  62 us (99%)
  between operations  0.8 us (1%)
    pallas_call x1, Pallas kernels, on_device(): pl.pallas_call(kernel, name='richardson', out_shape=pltpu.VMEM((2, rhs_co...  61 us

profile of v3, /device:TPU:1, one launch (start us, length us, event | category | flops | bytes accessed | tf_op | source)
XLA Modules:
  0.0 62.8 jit_solution(16213533756942972796)
XLA Ops:
  0.6 61.0 %richardson.1.result = f32[2,256,512]{2,1,0:T(8,128)S(1)} custom-call(f32[256,1024]{1,0:T(8,128)} %rhs_hbm.1, f32[256,512]{1,0:T(8,128)} %g_hbm.1, f32[2,128,8,512]{3,2,1,0:T(8,128)} %v_hbm.1, f32[2,128,8,512]{3,2,1,0:T(8,128)} %u_hbm.1, s32[2,128]{1,0:T(2,128)} %bitcast.1, f32[512,512]{1,0:T(8,128)} %d_hbm.1, f32[512,512]{1,0:T(8,128)} %di_hbm.1), custom_call_target="tpu_custom_call" | custom-call | tf_op jit(solution)/shard_map/richardson/pallas_call | solution.py:298
  61.7 1.0 %finish.1 = (f32[256,512]{1,0:T(8,128)}, f32[256,512]{1,0:T(8,128)}) custom-call(f32[2,256,512]{2,1,0:T(8,128)S(1)} %richardson.1.result), custom_call_target="tpu_custom_call" | custom-call | tf_op jit(solution)/shard_map/finish/pallas_call | solution.py:344

commit v4 on v3

--- a/solution.py
+++ b/solution.py
@@ -11,6 +11,8 @@
 CHUNK = 128
 MB = 1024
 EARLY = 40
+SHARED = 32
+LATE = 64 - SHARED
 
 
 SHIFTS = [(-(a + b) % 4, (a + 2 * b + c) % 4, a) for c in range(4) for b in range(4) for a in range(4)]
@@ -24,8 +26,8 @@
 def kernel(
     rhs_hbm, g_hbm, v_hbm, u_hbm, ranks_hbm, d_hbm, di_hbm, result,
     gin, rin, vf, vh, vl, uf, uth, utl, df, dh, dl, dif, dih, dil,
-    rhs, state, peer, dense, low, low_in, part, send, recv, wide,
-    ranks, targets, sources, load_sem, send_sem, recv_sem, g_send, g_recv, l_send, l_recv,
+    rhs, state, peer, dense, low, low_in, part, send, recv, wide, uf_peer, uth_peer, utl_peer, recv_last,
+    ranks, targets, sources, load_sem, send_sem, recv_sem, g_send, g_recv, l_send, l_recv, u_send, u_recv, last_recv,
 ):
     row = lax.axis_index("row")
     pan = lax.axis_index("pan")
@@ -118,7 +120,8 @@
         )
 
     def all_messages(slot, late):
-        first, count = (EARLY, 64 - EARLY) if late else (1, EARLY - 1)
+        cut = SHARED if slot == 3 else EARLY
+        first, count = (cut, 64 - cut) if late else (1, cut - 1)
         return pltpu.make_async_remote_copy(
             src_ref=send.at[slot, pl.ds(first, count)],
             dst_ref=recv.at[slot, pl.ds(first, count)],
@@ -152,6 +155,47 @@
     def scatter(slot):
         in_order(lambda n: message(slot, n, targets[n]).start())
         recv[slot, 0] = send[slot, row]
+
+    def last_message(n, target, kind):
+        core = (pan, other)[kind]
+        return pltpu.make_async_remote_copy(
+            src_ref=send.at[3, target, :, core],
+            dst_ref=recv_last.at[kind, n - SHARED],
+            send_sem=send_sem.at[3],
+            recv_sem=last_recv.at[kind],
+            device_id=(target, core),
+            device_id_type=MESH,
+        )
+
+    def all_last(kind):
+        return pltpu.make_async_remote_copy(
+            src_ref=recv_last.at[kind],
+            dst_ref=recv_last.at[kind],
+            send_sem=send_sem.at[3],
+            recv_sem=last_recv.at[kind],
+            device_id=(row, other),
+            device_id_type=MESH,
+        )
+
+    def scatter_last():
+        for n in range(1, 4):
+            message(3, n, targets[n]).start()
+
+        def early(m, carry):
+            for n in range(4):
+                message(3, 4 * m + n, targets[4 * m + n]).start()
+            return carry
+
+        lax.fori_loop(1, SHARED // 4, early, 0)
+
+        def late(m, carry):
+            for n in range(4):
+                for kind in range(2):
+                    last_message(4 * m + n, targets[4 * m + n], kind).start()
+            return carry
+
+        lax.fori_loop(SHARED // 4, 16, late, 0)
+        recv[3, 0] = send[3, row]
 
     def scatter_half(slot, tile, beside=None):
         def visit(n):
@@ -207,6 +251,22 @@
     for n in range(64):
         sources[n] = shifted(n, -1)
     load_u.wait()
+
+    def u_copy(m):
+        return pltpu.make_async_remote_copy(
+            src_ref=uf.at[other, pl.ds(2 * sources[SHARED + m], 2)],
+            dst_ref=uf_peer.at[m],
+            send_sem=u_send,
+            recv_sem=u_recv,
+            device_id=(row, other),
+            device_id_type=MESH,
+        )
+
+    def start_u(m, carry):
+        u_copy(m).start()
+        return carry
+
+    lax.fori_loop(0, LATE, start_u, 0)
     for i in range(2):
         def turn(m, carry):
             pieces = []
@@ -221,6 +281,19 @@
             return carry
 
         lax.fori_loop(0, 8, turn, 0)
+    all_u = pltpu.make_async_remote_copy(
+        src_ref=uf_peer,
+        dst_ref=uf_peer,
+        send_sem=u_send,
+        recv_sem=u_recv,
+        device_id=(row, other),
+        device_id_type=MESH,
+    )
+    all_u.wait_recv()
+    for m in range(LATE // 8):
+        hi, lo = split(uf_peer[8 * m:8 * m + 8].reshape(128, width).T)
+        uth_peer[:, 128 * m:128 * m + 128] = hi
+        utl_peer[:, 128 * m:128 * m + 128] = lo
     load_d.wait()
     dh[...], dl[...] = split(df[...])
     load_di.wait()
@@ -237,7 +310,8 @@
         subtract_dense(0, q)
 
     def low_rank(slot, i, late):
-        first, count = (EARLY, 64 - EARLY) if late else (0, EARLY)
+        cut = SHARED if slot == 3 else EARLY
+        first, count = (cut, 64 - cut) if late else (0, cut)
         columns = pl.ds(16 * first, 16 * count)
         operand = wide.at[columns]
         widen(operand, recv[slot, first:first + count, :, i].reshape(16 * count, CHUNK))
@@ -258,6 +332,25 @@
         widen(operand, residual)
         return residual, state[it, q] + product(dih, dil, operand)
 
+    def advance_last():
+        all_messages(3, 0).wait_recv()
+        low[3] = low_rank(3, other, 0)
+        low_copy(3).start()
+        own = dense[1] - low_rank(3, pan, 0)
+        low_copy(3).wait_recv()
+        own = own - low_in[3]
+        late = pl.ds(16 * SHARED, 16 * LATE)
+        operand = wide.at[pl.ds(0, 16 * LATE)]
+        all_last(0).wait_recv()
+        widen(operand, recv_last[0].reshape(16 * LATE, CHUNK))
+        own = own - product(uth.at[pan, :, late], utl.at[pan, :, late], operand)
+        all_last(1).wait_recv()
+        widen(operand, recv_last[1].reshape(16 * LATE, CHUNK))
+        residual = own - product(uth_peer, utl_peer, operand)
+        operand = wide.at[pl.ds(0, width)]
+        widen(operand, residual)
+        return residual, state[1, 1] + product(dih, dil, operand)
+
     for q in range(2):
         residual, guess = advance(0, q)
         state[1, q] = guess
@@ -265,14 +358,18 @@
         project(2 + q, pan, guess)
         guess_copy(1, q).wait_recv()
         project(2 + q, other, peer[1, q])
-        scatter(2 + q)
+        if q == 0:
+            scatter(2)
+        else:
+            scatter_last()
         subtract_dense(1, q)
 
     for q in range(2):
-        residual, guess = advance(1, q)
+        residual, guess = advance(1, 0) if q == 0 else advance_last()
         result[0, q * CHUNK:(q + 1) * CHUNK] = guess.T
         result[1, q * CHUNK:(q + 1) * CHUNK] = residual.T
 
+    all_u.wait_send()
     for slot in range(4):
         for late in range(2):
             all_messages(slot, late).wait_send()
@@ -326,6 +423,10 @@
             pltpu.VMEM((4, 64, tiles, tiles, part, CHUNK), F32),
             pltpu.VMEM((4, 64, tiles, tiles, part, CHUNK), F32),
             pltpu.VMEM((1024, 2 * CHUNK), BF16),
+            pltpu.VMEM((LATE, tiles, part, width), F32),
+            pltpu.VMEM((width, LATE * tiles * part), BF16),
+            pltpu.VMEM((width, LATE * tiles * part), BF16),
+            pltpu.VMEM((2, LATE, tiles, part, CHUNK), F32),
             pltpu.SMEM(tile_ranks.shape[::-1], jnp.int32),
             pltpu.SMEM((64,), jnp.int32),
             pltpu.SMEM((64,), jnp.int32),
@@ -336,6 +437,9 @@
             pltpu.SemaphoreType.DMA((4,)),
             pltpu.SemaphoreType.DMA((4,)),
             pltpu.SemaphoreType.DMA((4,)),
+            pltpu.SemaphoreType.DMA,
+            pltpu.SemaphoreType.DMA,
+            pltpu.SemaphoreType.DMA((2,)),
         ],
         compiler_params=pltpu.CompilerParams(
             collective_id=0, has_side_effects=True, vmem_limit_bytes=58 << 20

time: 62.9 us -> 61.2 us (0.973)
  Pallas kernels: 62 us -> 60.2 us
    pallas_call x1, Pallas kernels: 61 us -> 59.3 us  [on_device(): pl.pallas_call(kernel, name='richardson', out_shape=pltpu.VMEM((2, rhs_co...]
where the time goes in v4:
time: 61.2 us; the launch traced here: 61 us
  Pallas kernels  60.2 us (98%)
  between operations  0.8 us (1%)
    pallas_call x1, Pallas kernels, on_device(): pl.pallas_call(kernel, name='richardson', out_shape=pltpu.VMEM((2, rhs_co...  59.3 us

profile of v4, /device:TPU:1, one launch (start us, length us, event | category | flops | bytes accessed | tf_op | source)
XLA Modules:
  0.0 61.0 jit_solution(17919203452061112779)
XLA Ops:
  0.6 59.3 %richardson.1.result = f32[2,256,512]{2,1,0:T(8,128)S(1)} custom-call(f32[256,1024]{1,0:T(8,128)} %rhs_hbm.1, f32[256,512]{1,0:T(8,128)} %g_hbm.1, f32[2,128,8,512]{3,2,1,0:T(8,128)} %v_hbm.1, f32[2,128,8,512]{3,2,1,0:T(8,128)} %u_hbm.1, s32[2,128]{1,0:T(2,128)} %bitcast.1, f32[512,512]{1,0:T(8,128)} %d_hbm.1, f32[512,512]{1,0:T(8,128)} %di_hbm.1), custom_call_target="tpu_custom_call" | custom-call | tf_op jit(solution)/shard_map/richardson/pallas_call | solution.py:395
  59.9 1.0 %finish.1 = (f32[256,512]{1,0:T(8,128)}, f32[256,512]{1,0:T(8,128)}) custom-call(f32[2,256,512]{2,1,0:T(8,128)S(1)} %richardson.1.result), custom_call_target="tpu_custom_call" | custom-call | tf_op jit(solution)/shard_map/finish/pallas_call | solution.py:448

commit v5 on v4

--- a/solution.py
+++ b/solution.py
@@ -142,15 +142,12 @@
         )
 
     def in_order(visit):
-        for n in range(1, 4):
-            visit(n)
-
         def body(m, carry):
-            for n in range(4):
-                visit(4 * m + n)
+            for n in range(3):
+                visit(1 + 3 * m + n)
             return carry
 
-        lax.fori_loop(1, 16, body, 0)
+        lax.fori_loop(0, 21, body, 0)
 
     def scatter(slot):
         in_order(lambda n: message(slot, n, targets[n]).start())

time: 61.2 us -> 61.1 us (level)
  no operation moved by 1% of the time
where the time goes in v5:
time: 61.1 us; the launch traced here: 61 us
  Pallas kernels  60.2 us (99%)
  between operations  0.8 us (1%)
    pallas_call x1, Pallas kernels, on_device(): pl.pallas_call(kernel, name='richardson', out_shape=pltpu.VMEM((2, rhs_co...  59.2 us

profile of v5, /device:TPU:1, one launch (start us, length us, event | category | flops | bytes accessed | tf_op | source)
XLA Modules:
  0.0 61.0 jit_solution(15601219684907020511)
XLA Ops:
  0.6 59.2 %richardson.1.result = f32[2,256,512]{2,1,0:T(8,128)S(1)} custom-call(f32[256,1024]{1,0:T(8,128)} %rhs_hbm.1, f32[256,512]{1,0:T(8,128)} %g_hbm.1, f32[2,128,8,512]{3,2,1,0:T(8,128)} %v_hbm.1, f32[2,128,8,512]{3,2,1,0:T(8,128)} %u_hbm.1, s32[2,128]{1,0:T(2,128)} %bitcast.1, f32[512,512]{1,0:T(8,128)} %d_hbm.1, f32[512,512]{1,0:T(8,128)} %di_hbm.1), custom_call_target="tpu_custom_call" | custom-call | tf_op jit(solution)/shard_map/richardson/pallas_call | solution.py:392
  59.9 1.0 %finish.1 = (f32[256,512]{1,0:T(8,128)}, f32[256,512]{1,0:T(8,128)}) custom-call(f32[2,256,512]{2,1,0:T(8,128)S(1)} %richardson.1.result), custom_call_target="tpu_custom_call" | custom-call | tf_op jit(solution)/shard_map/finish/pallas_call | solution.py:445

commit v6 on v5

--- a/solution.py
+++ b/solution.py
@@ -54,8 +54,6 @@
     own_columns = pl.ds(pl.multiple_of(pan * width, width), width)
     load_r = pltpu.make_async_copy(rhs_hbm.at[:, own_columns], rin, load_sem.at[6])
     load_ranks = pltpu.make_async_copy(ranks_hbm, ranks, load_sem.at[7])
-    load_g.start()
-    load_v[0].start()
 
     barrier = pltpu.get_barrier_semaphore()
     pl.semaphore_signal(barrier, inc=1, device_id=(row, other), device_id_type=MESH)
@@ -67,14 +65,15 @@
         return carry
 
     lax.fori_loop(1, 64, greet, 0, unroll=9)
+    load_g.start()
+    load_v[0].start()
     load_ranks.start()
     load_v[1].start()
     for n in range(1, 64):
         targets[n] = shifted(n, 1)
 
     load_g.wait()
-    for q in range(2):
-        state[0, q] = gin[q * CHUNK:(q + 1) * CHUNK, :].T
+    state[0, 0] = gin[:CHUNK, :].T
 
     components = lax.broadcasted_iota(jnp.int32, (8, width), 0) + 8 * pan
 
@@ -231,12 +230,13 @@
     lax.fori_loop(0, 64, prepare_own, 0, unroll=4)
     project(0, pan, state[0, 0])
     pl.semaphore_wait(barrier, 64)
-    for q in range(2):
-        guess_copy(0, q).start()
+    guess_copy(0, 0).start()
     load_v[1].wait()
     for load in (load_d, load_di, load_r, load_u):
         load.start()
     scatter_half(0, pan, lambda d: prepare_v(other, d))
+    state[0, 1] = gin[CHUNK:, :].T
+    guess_copy(0, 1).start()
     guess_copy(0, 0).wait_recv()
     project(0, other, peer[0, 0])
     scatter_half(0, other)

time: 61.1 us -> 61.5 us (level)
  no operation moved by 1% of the time
where the time goes in v6:
time: 61.5 us; the launch traced here: 61.4 us
  Pallas kernels  60.6 us (99%)
  between operations  0.8 us (1%)
    pallas_call x1, Pallas kernels, on_device(): pl.pallas_call(kernel, name='richardson', out_shape=pltpu.VMEM((2, rhs_co...  59.6 us

profile of v6, /device:TPU:1, one launch (start us, length us, event | category | flops | bytes accessed | tf_op | source)
XLA Modules:
  0.0 61.4 jit_solution(11922528004868421025)
XLA Ops:
  0.6 59.6 %richardson.1.result = f32[2,256,512]{2,1,0:T(8,128)S(1)} custom-call(f32[256,1024]{1,0:T(8,128)} %rhs_hbm.1, f32[256,512]{1,0:T(8,128)} %g_hbm.1, f32[2,128,8,512]{3,2,1,0:T(8,128)} %v_hbm.1, f32[2,128,8,512]{3,2,1,0:T(8,128)} %u_hbm.1, s32[2,128]{1,0:T(2,128)} %bitcast.1, f32[512,512]{1,0:T(8,128)} %d_hbm.1, f32[512,512]{1,0:T(8,128)} %di_hbm.1), custom_call_target="tpu_custom_call" | custom-call | tf_op jit(solution)/shard_map/richardson/pallas_call | solution.py:392
  60.3 1.0 %finish.1 = (f32[256,512]{1,0:T(8,128)}, f32[256,512]{1,0:T(8,128)}) custom-call(f32[2,256,512]{2,1,0:T(8,128)S(1)} %richardson.1.result), custom_call_target="tpu_custom_call" | custom-call | tf_op jit(solution)/shard_map/finish/pallas_call | solution.py:445

commit v7 on v5

--- a/solution.py
+++ b/solution.py
@@ -10,7 +10,7 @@
 BF16 = jnp.bfloat16
 CHUNK = 128
 MB = 1024
-EARLY = 40
+EARLY = 48
 SHARED = 32
 LATE = 64 - SHARED
 

time: 61.1 us -> 61.1 us (level)
  no operation moved by 1% of the time
where the time goes in v7:
time: 61.1 us; the launch traced here: 61 us
  Pallas kernels  60.2 us (99%)
  between operations  0.8 us (1%)
    pallas_call x1, Pallas kernels, on_device(): pl.pallas_call(kernel, name='richardson', out_shape=pltpu.VMEM((2, rhs_co...  59.2 us

profile of v7, /device:TPU:1, one launch (start us, length us, event | category | flops | bytes accessed | tf_op | source)
XLA Modules:
  0.0 61.0 jit_solution(8885693683611455796)
XLA Ops:
  0.6 59.2 %richardson.1.result = f32[2,256,512]{2,1,0:T(8,128)S(1)} custom-call(f32[256,1024]{1,0:T(8,128)} %rhs_hbm.1, f32[256,512]{1,0:T(8,128)} %g_hbm.1, f32[2,128,8,512]{3,2,1,0:T(8,128)} %v_hbm.1, f32[2,128,8,512]{3,2,1,0:T(8,128)} %u_hbm.1, s32[2,128]{1,0:T(2,128)} %bitcast.1, f32[512,512]{1,0:T(8,128)} %d_hbm.1, f32[512,512]{1,0:T(8,128)} %di_hbm.1), custom_call_target="tpu_custom_call" | custom-call | tf_op jit(solution)/shard_map/richardson/pallas_call | solution.py:392
  59.9 1.0 %finish.1 = (f32[256,512]{1,0:T(8,128)}, f32[256,512]{1,0:T(8,128)}) custom-call(f32[2,256,512]{2,1,0:T(8,128)S(1)} %richardson.1.result), custom_call_target="tpu_custom_call" | custom-call | tf_op jit(solution)/shard_map/finish/pallas_call | solution.py:445
